TPU v7x, 128 devices: a whole 4x4x4 slice. The times are simulated.
128 devices in a mesh: req: 8 (over y, core), tok: 16 (over x, z).
Axes of the slice: x: 4, y: 4, z: 4, core: 2. Of those that a mesh axis runs over, the one named last changes fastest.
Arguments:
- layer_input: bfloat16 [16384, 2048], P(('req', 'tok')), may hold values from -12 to 12
- q_in: bfloat16 [16384, 2048], P(('req', 'tok')), may hold values from -10 to 10
- k_in: bfloat16 [16384, 2048], P(('req', 'tok')), may hold values from -10 to 10
- v_in: bfloat16 [16384, 2048], P(('req', 'tok')), may hold values from -6 to 6
- segment_ids: int32 [8, 2048], P('req'), may hold values from 0 to 3, never falling along the last dimension, each value on 1 to 1024 neighbouring positions
- lambda_parts: float32 [4, 128], replicated, may hold values from -0.8 to 0.8
- out_weight: bfloat16 [2048, 2048], replicated, may hold values from -0.125 to 0.125
- ffn_gain: float32 [2048], replicated, may hold values from 0.1 to 1.9
- gate_weight: bfloat16 [2048, 5632], P(None, 'req'), may hold values from -0.125 to 0.125
- up_weight: bfloat16 [2048, 5632], P(None, 'req'), may hold values from -0.125 to 0.125
- down_weight: bfloat16 [5632, 2048], P('req'), may hold values from -0.078125 to 0.078125
- next_gain: float32 [2048], replicated, may hold values from 0.1 to 1.9
- qkv_weight: bfloat16 [2048, 6144], P(None, 'req'), may hold values from -0.125 to 0.125
- page_owner: int32 [8, 256], P('req'), may hold values from 0 to 15, as said below
- page_slot: int32 [8, 256], P('req'), may hold values from 0 to 15, as said below
Outputs:
- layer_output: bfloat16 [16384, 2048], P(('req', 'tok'))
- q_next: bfloat16 [16384, 2048], P(('req', 'tok'))
- page_cache: bfloat16 [2048, 8, 4096], P(('req', 'tok'))
Inputs may be any that keep to these rules, and one draw needn't show every extreme that they name: `segment_ids`: segment numbers never fall along a group; each of the 4 prompts of a group has 1 to 1024 tokens, one exactly 1024. `page_owner`: the 16 pages of each device name every device of its request group as owner exactly once. `page_slot`: within a request group every pair of owner and slot is named by exactly one page.
All inputs are finite; a program needn't handle non-finite values.
Results may differ from a plain program's by a relative error of at most 0.017.
Values may be sent and summed in bfloat16 or wider, within the bound.
A program may use at most 192 MiB of HBM per device.

v0:
```python
import math
import jax
import jax.numpy as jnp
from jax import lax
from jax.sharding import PartitionSpec as P

HEADS = 8
PAGE = 8
NEG_FILL = -1e30
LAMBDA_INIT = 0.2
EPSILON = 1e-05
MAX_SEG = 1024


def rms_rows(values):
    return values * lax.rsqrt(jnp.mean(values * values, axis=-1, keepdims=True) + EPSILON)


def lambda_value(lambda_parts):
    first_term = jnp.exp(jnp.sum(lambda_parts[0] * lambda_parts[1]))
    second_term = jnp.exp(jnp.sum(lambda_parts[2] * lambda_parts[3]))
    return first_term - second_term + LAMBDA_INIT


def body(
    layer_input,
    q_in,
    k_in,
    v_in,
    segment_ids,
    lambda_parts,
    out_weight,
    ffn_gain,
    gate_weight,
    up_weight,
    down_weight,
    next_gain,
    qkv_weight,
    page_owner,
    page_slot,
):
    row_count = q_in.shape[0]
    feat_width = q_in.shape[1]
    head_dim = feat_width // (2 * HEADS)
    peer_count = lax.axis_size("tok")
    tok_place = lax.axis_index("tok")
    seg_row = segment_ids[0]
    first_row = tok_place * row_count
    query_places = first_row + jnp.arange(row_count)
    query_segs = lax.dynamic_slice_in_dim(seg_row, first_row, row_count)
    lambda_mix = lambda_value(lambda_parts)
    score_scale = 1.0 / math.sqrt(head_dim)
    query_split = q_in.reshape(row_count, HEADS, 2, head_dim)
    run_max = jnp.full((HEADS, 2, row_count), NEG_FILL, jnp.float32)
    back = -(-(MAX_SEG - 1) // row_count)
    own_kv = jnp.concatenate([k_in, v_in], axis=1)
    all_kv = lax.all_gather(own_kv, "tok", axis=0, tiled=True)
    padded_kv = jnp.concatenate(
        [jnp.zeros((back * row_count, 2 * feat_width), all_kv.dtype), all_kv], axis=0
    )
    window = lax.dynamic_slice_in_dim(padded_kv, first_row, (back + 1) * row_count, 0)
    piece_len = window.shape[0]
    key_rows = window[:, :feat_width]
    value_rows = window[:, feat_width:]
    key_split = key_rows.reshape(piece_len, HEADS, 2, head_dim)
    value_split = value_rows.reshape(piece_len, HEADS, 2 * head_dim)
    key_places = (tok_place - back) * row_count + jnp.arange(piece_len)
    key_segs = jnp.take(seg_row, jnp.clip(key_places, 0, seg_row.shape[0] - 1))
    visible = (
        (key_places[None, :] >= 0)
        & (key_segs[None, :] == query_segs[:, None])
        & (key_places[None, :] <= query_places[:, None])
    )
    scores = (
        jnp.einsum("qhmd,khmd->hmqk", query_split, key_split, preferred_element_type=jnp.float32)
        * score_scale
    )
    scores = jnp.where(visible, scores, NEG_FILL)
    new_max = jnp.maximum(run_max, jnp.max(scores, axis=-1))
    weights = jnp.where(visible, jnp.exp(scores - new_max[..., None]), 0.0)
    totals = jnp.sum(weights, axis=-1)
    weighted = jnp.einsum(
        "hmqk,khe->hmqe",
        weights.astype(jnp.bfloat16),
        value_split,
        preferred_element_type=jnp.float32,
    )
    run_max, totals, weighted = (new_max, totals, weighted)
    map_outputs = weighted / totals[..., None]
    difference = map_outputs[:, 0] - lambda_mix * map_outputs[:, 1]
    head_outputs = rms_rows(difference) * (1.0 - LAMBDA_INIT)
    attention = (
        jnp.transpose(head_outputs, (1, 0, 2)).reshape(row_count, feat_width).astype(jnp.bfloat16)
    )
    residual_mid = (
        layer_input.astype(jnp.float32)
        + jnp.dot(attention, out_weight, preferred_element_type=jnp.float32)
    ).astype(jnp.bfloat16)
    gathered = lax.all_gather(residual_mid, "req", axis=0, tiled=True)
    normed = (rms_rows(gathered.astype(jnp.float32)) * ffn_gain).astype(jnp.bfloat16)
    gate_proj = jnp.dot(normed, gate_weight, preferred_element_type=jnp.float32)
    up_proj = jnp.dot(normed, up_weight, preferred_element_type=jnp.float32)
    hidden = (jax.nn.silu(gate_proj) * up_proj).astype(jnp.bfloat16)
    ffn_own = lax.psum_scatter(
        jnp.dot(hidden, down_weight, preferred_element_type=jnp.float32).astype(jnp.bfloat16),
        "req",
        scatter_dimension=0,
        tiled=True,
    ).astype(jnp.float32)
    layer_output = (residual_mid.astype(jnp.float32) + ffn_own).astype(jnp.bfloat16)
    next_normed = (rms_rows(layer_output.astype(jnp.float32)) * next_gain).astype(jnp.bfloat16)
    projected_cols = jnp.dot(
        lax.all_gather(next_normed, "req", axis=0, tiled=True),
        qkv_weight,
        preferred_element_type=jnp.float32,
    ).astype(jnp.bfloat16)
    projected = lax.all_to_all(projected_cols, "req", split_axis=0, concat_axis=1, tiled=True)
    q_next = projected[:, :feat_width]
    pages_dev = row_count // PAGE
    per_owner = pages_dev // peer_count
    key_values = projected[:, feat_width:].reshape(pages_dev, PAGE, 2 * feat_width)
    owner_all = page_owner[0].reshape(peer_count, pages_dev)
    slot_all = page_slot[0].reshape(peer_count, pages_dev)
    page_numbers = jnp.arange(pages_dev, dtype=jnp.int32)
    my_owners = lax.dynamic_index_in_dim(owner_all, tok_place, 0, keepdims=False)
    send_order = jnp.argsort(my_owners * pages_dev + page_numbers)
    outgoing = key_values[send_order].reshape(peer_count, per_owner, PAGE, 2 * feat_width)
    incoming = lax.all_to_all(outgoing, "tok", split_axis=0, concat_axis=0, tiled=True)
    rank_keys = jnp.where(
        owner_all == tok_place, page_numbers[None, :], pages_dev + page_numbers[None, :]
    )
    chosen_pages = jnp.argsort(rank_keys, axis=1)[:, :per_owner]
    slot_list = jnp.take_along_axis(slot_all, chosen_pages, axis=1).reshape(pages_dev)
    page_cache = (
        jnp.zeros((pages_dev, PAGE, 2 * feat_width), jnp.bfloat16)
        .at[slot_list]
        .set(incoming.reshape(pages_dev, PAGE, 2 * feat_width))
    )
    return (layer_output, q_next, page_cache)


def solution(mesh):
    in_specs = (
        P(("req", "tok"), None),
        P(("req", "tok"), None),
        P(("req", "tok"), None),
        P(("req", "tok"), None),
        P("req", None),
        P(),
        P(),
        P(),
        P(None, "req"),
        P(None, "req"),
        P("req", None),
        P(),
        P(None, "req"),
        P("req", None),
        P("req", None),
    )
    out_specs = (P(("req", "tok"), None), P(("req", "tok"), None), P(("req", "tok"), None, None))
    return jax.shard_map(body, mesh=mesh, in_specs=in_specs, out_specs=out_specs, check_vma=False)
```

profile of v0, /device:TPU:0, one launch (start us, length us, event | category | flops | bytes accessed | tf_op | source)
XLA Modules:
  0.0 369.7 jit_solution(3113207393178205079)
XLA Ops:
  7.2 2.2 copy.38
  11.5 2.2 pad_maximum_fusion
  13.8 2.2 reshape.141
  18.0 6.5 %gather_fusion = s32[1152]{0:T(1024)S(1)} fusion(s32[2048]{0:T(1024)S(1)} %bitcast.64, s32[2048]{0:T(1024)S(1)} %pad_clamp_fusion), kind=kCustom, calls=%fused_computation | custom fusion | bytes 13824 | tf_op jit(solution)/shard_map/jit(_take)/gather | solution.py:68
  25.6 112.0 %all-gather.4.cloned.1.call-done = bf16[2048,4096]{0,1:T(8,128)(2,1)} async-done(((bf16[128,4096]{0,1:T(8,128)(2,1)}), bf16[2048,4096]{0,1:T(8,128)(2,1)}) %all-gather.4.cloned.1.call-update) | async-done | bytes 16777232 | tf_op jit(solution)/shard_map/all_gather | solution.py:57
  137.5 5.1 %pad_dynamic-slice_fusion.1 = (bf16[1152,2048]{0,1:T(8,128)(2,1)}, bf16[1152,2048]{0,1:T(8,128)(2,1)S(1)}) fusion(s32[]{:T(128)S(6)} %select_n.70, s32[]{:T(128)S(6)} %add.181, bf16[2048,4096]{0,1:T(8,128)(2,1)} %all-gather.4.cloned.1.call-done), kind=kLoop, calls=%fused_computation.5 | loop fusion | bytes 26214408 | tf_op jit(solution)/shard_map/slice | solution.py:64
  142.6 2.5 fusion.3
  145.1 2.3 fusion.4
  148.7 8.3 %broadcast_divide_fusion = f32[8,2,128,256]{3,2,1,0:T(8,128)S(1)} fusion(f32[8,2,128]{2,1,0:T(2,128)S(1)} %fusion.4, bf16[1152,8,256,1]{0,2,3,1:T(8,128)(2,1)} %bitcast.68, f32[8,2,1152,128]{3,2,1,0:T(8,128)} %copy-done.2, f32[8,2,128]{2,1,0:T(2,128)S(1)} %broadcast_maximum_fusion, pred[128,1152]{0,1:T(8,128)(4,1)S(1)} %compare_and_fusion), kind=kOutput, calls=%fused_computation.41 | convolution fusion | flops 1220280320 | bytes 16416768 | tf_op jit(solution)/shard_map/hmqk,khe->hmqe/dot_general | solution.py:82
  158.3 2.0 copy.44
  160.3 5.7 %fusion.13 = bf16[128,2048]{1,0:T(8,128)(2,1)} fusion(bf16[128,2048]{0,1:T(8,128)(2,1)} %bitcast.70, bf16[2048,2048]{1,0:T(8,128)(2,1)} %param.21, bf16[128,2048]{1,0:T(8,128)(2,1)} %param.15), kind=kOutput, calls=%fused_computation.25 | convolution fusion | flops 1074528256 | bytes 9961472 | tf_op jit(solution)/shard_map/dot_general | solution.py:97
  166.3 33.9 %all-gather.6.cloned.1.call-done = bf16[1024,2048]{1,0:T(8,128)(2,1)} async-done(((bf16[128,2048]{1,0:T(8,128)(2,1)}), bf16[1024,2048]{1,0:T(8,128)(2,1)}) %all-gather.6.cloned.1.call-update) | async-done | bytes 4194320 | tf_op jit(solution)/shard_map/all_gather | solution.py:99
  200.1 3.2 fusion
  203.6 6.7 %fusion.15 = f32[1024,704]{0,1:T(8,128)} fusion(bf16[2048,704]{0,1:T(8,128)(2,1)} %param.23, bf16[1024,2048]{1,0:T(8,128)(2,1)S(1)} %copy-done.4, f32[2048]{0:T(1024)S(1)} %copy-done.11, f32[1024]{0:T(1024)S(1)} %add_rsqrt_fusion), kind=kOutput, calls=%fused_computation.29 | convolution fusion | flops 2961178624 | bytes 9973760 | tf_op jit(solution)/shard_map/dot_general | solution.py:101
  210.3 12.4 %convolution_convert_fusion = bf16[1024,2048]{1,0:T(8,128)(2,1)} fusion(bf16[704,2048]{1,0:T(8,128)(2,1)} %param.25, f32[1024,704]{0,1:T(8,128)} %fusion.15, bf16[2048,704]{0,1:T(8,128)(2,1)} %param.24, bf16[1024,2048]{1,0:T(8,128)(2,1)} %all-gather.6.cloned.1.call-done, f32[2048]{0:T(1024)S(1)} %copy-done.11, f32[1024]{0:T(1024)S(1)} %add_rsqrt_fusion), kind=kOutput, calls=%fused_computation.22 | convolution fusion | flops 5920391168 | bytes 17051648 | tf_op jit(solution)/shard_map/dot_general | solution.py:105
  222.8 37.9 %reduce-scatter.2.cloned.1.call-done = bf16[128,2048]{1,0:T(8,128)(2,1)} async-done(((bf16[1024,2048]{1,0:T(8,128)(2,1)}), bf16[128,2048]{1,0:T(8,128)(2,1)}) %reduce-scatter.2.cloned.1.call-update) | async-done | bytes 524304 | tf_op jit(solution)/shard_map/reduce_scatter | solution.py:104
  263.9 31.2 %all-gather.8.cloned.1.call-done = bf16[1024,2048]{1,0:T(8,128)(2,1)} async-done(((bf16[128,2048]{1,0:T(8,128)(2,1)}), bf16[1024,2048]{1,0:T(8,128)(2,1)}) %all-gather.8.cloned.1.call-update) | async-done | bytes 4194320 | tf_op jit(solution)/shard_map/all_gather | solution.py:113
  295.1 6.8 %convolution_convert_fusion.1 = bf16[1024,768]{1,0:T(8,128)(2,1)} fusion(bf16[1024,2048]{1,0:T(8,128)(2,1)} %all-gather.8.cloned.1.call-done, bf16[2048,768]{1,0:T(8,128)(2,1)S(1)} %copy-done), kind=kOutput, calls=%fused_computation.26 | convolution fusion | flops 3222011904 | bytes 8912896 | tf_op jit(solution)/shard_map/dot_general | solution.py:112
  301.8 4.3 %all-to-all-start = ((bf16[8,128,768]{2,1,0:T(8,128)(2,1)}), bf16[8,128,768]{2,1,0:T(8,128)(2,1)}, u32[]{:S(2)}, u32[]{:S(2)}) async-start(bf16[8,128,768]{2,1,0:T(8,128)(2,1)} %bitcast.71), calls=%async_computation.1 | async-start | bytes 3145728 | tf_op jit(solution)/shard_map/all_to_all | solution.py:117
  309.5 18.2 %all-to-all-done = bf16[8,128,768]{2,1,0:T(8,128)(2,1)} async-done(((bf16[8,128,768]{2,1,0:T(8,128)(2,1)}), bf16[8,128,768]{2,1,0:T(8,128)(2,1)}, u32[]{:S(2)}, u32[]{:S(2)}) %all-to-all-start) | async-done | bytes 1572896 | tf_op jit(solution)/shard_map/all_to_all | solution.py:117
  331.5 2.8 gather_fusion.1
  334.3 7.0 %all-to-all-start.1 = ((bf16[16,1,8,4096]{3,2,1,0:T(8,128)(2,1)}), bf16[16,1,8,4096]{3,2,1,0:T(8,128)(2,1)}, u32[]{:S(2)}, u32[]{:S(2)}) async-start(bf16[16,1,8,4096]{3,2,1,0:T(8,128)(2,1)} %bitcast.69), calls=%async_computation.2 | async-start | bytes 2097152 | tf_op jit(solution)/shard_map/all_to_all | solution.py:128
  344.7 14.1 %all-to-all-done.1 = bf16[16,1,8,4096]{3,2,1,0:T(8,128)(2,1)} async-done(((bf16[16,1,8,4096]{3,2,1,0:T(8,128)(2,1)}), bf16[16,1,8,4096]{3,2,1,0:T(8,128)(2,1)}, u32[]{:S(2)}, u32[]{:S(2)}) %all-to-all-start.1) | async-done | bytes 1048608 | tf_op jit(solution)/shard_map/all_to_all | solution.py:128
  359.8 3.4 scatter_fusion
  (74 shorter events, 21.9 us)
Async XLA Ops:
  7.2 287.9 %copy-start = (bf16[2048,768]{1,0:T(8,128)(2,1)S(1)}, bf16[2048,768]{1,0:T(8,128)(2,1)}, u32[]{:S(2)}) copy-start(bf16[2048,768]{1,0:T(8,128)(2,1)} %param.27) | copy-start | bytes 9437188
  7.2 8.8 %copy-start.8 = (f32[4,128]{1,0:T(4,128)S(1)}, f32[4,128]{1,0:T(4,128)}, u32[]{:S(2)}) copy-start(f32[4,128]{1,0:T(4,128)} %param.20) | copy-start | bytes 6148
  7.2 10.8 %copy-start.1 = (s32[1,2048]{1,0:T(1,128)S(1)}, s32[1,2048]{1,0:T(1,128)}, u32[]{:S(2)}) copy-start(s32[1,2048]{1,0:T(1,128)} %param.19) | copy-start | bytes 24580
  7.2 130.3 %all-gather.4.cloned.1.call-start = ((), (), s32[]{:S(2)}) async-start(), calls=%async_computation.3 | async-start | bytes 17825792 | tf_op jit(solution)/shard_map/all_gather | solution.py:57
  13.7 186.4 %all-gather.6.cloned.1.call-start = ((), (), s32[]{:S(2)}) async-start(), calls=%async_computation.4 | async-start | bytes 4718592 | tf_op jit(solution)/shard_map/all_gather | solution.py:99
  137.5 5.1 %copy-start.5 = (bf16[128,8,2,128]{3,2,1,0:T(2,128)(2,1)S(1)}, bf16[128,8,2,128]{3,2,1,0:T(2,128)(2,1)}, u32[]{:S(2)}) copy-start(bf16[128,8,2,128]{3,2,1,0:T(2,128)(2,1)} %reshape.141) | copy-start | bytes 1572868
  145.1 3.6 copy-start.2
  166.0 37.4 %copy-start.11 = (f32[2048]{0:T(1024)S(1)}, f32[2048]{0:T(1024)}, u32[]{:S(2)}) copy-start(f32[2048]{0:T(1024)} %param.22) | copy-start | bytes 24580
  166.0 94.6 %reduce-scatter.2.cloned.1.call-start = ((), (), s32[]{:S(2)}) async-start(), calls=%async_computation.5 | async-start | bytes 4718592 | tf_op jit(solution)/shard_map/reduce_scatter | solution.py:104
  200.1 3.4 copy-start.4
  222.7 40.2 %copy-start.7 = (f32[2048]{0:T(1024)S(1)}, f32[2048]{0:T(1024)}, u32[]{:S(2)}) copy-start(f32[2048]{0:T(1024)} %param.26) | copy-start | bytes 24580
  222.7 72.4 %all-gather.8.cloned.1.call-start = ((), (), s32[]{:S(2)}) async-start(), calls=%async_computation.6 | async-start | bytes 4718592 | tf_op jit(solution)/shard_map/all_gather | solution.py:113
  262.1 0.8 copy-start.6
  263.9 42.8 %copy-start.9 = (s32[1,256]{1,0:T(1,128)S(1)}, s32[1,256]{1,0:T(1,128)}, u32[]{:S(2)}) copy-start(s32[1,256]{1,0:T(1,128)} %param.28) | copy-start | bytes 3076
  263.9 43.6 %copy-start.10 = (s32[1,256]{1,0:T(1,128)S(1)}, s32[1,256]{1,0:T(1,128)}, u32[]{:S(2)}) copy-start(s32[1,256]{1,0:T(1,128)} %param.29) | copy-start | bytes 3076
  301.8 25.9 %all-to-all-start = ((bf16[8,128,768]{2,1,0:T(8,128)(2,1)}), bf16[8,128,768]{2,1,0:T(8,128)(2,1)}, u32[]{:S(2)}, u32[]{:S(2)}) async-start(bf16[8,128,768]{2,1,0:T(8,128)(2,1)} %bitcast.71), calls=%async_computation.1 | async-start | bytes 3145728 | tf_op jit(solution)/shard_map/all_to_all | solution.py:117
  329.3 1.2 copy-start.3
  334.3 24.4 %all-to-all-start.1 = ((bf16[16,1,8,4096]{3,2,1,0:T(8,128)(2,1)}), bf16[16,1,8,4096]{3,2,1,0:T(8,128)(2,1)}, u32[]{:S(2)}, u32[]{:S(2)}) async-start(bf16[16,1,8,4096]{3,2,1,0:T(8,128)(2,1)} %bitcast.69), calls=%async_computation.2 | async-start | bytes 2097152 | tf_op jit(solution)/shard_map/all_to_all | solution.py:128
Sparse Core Ops, SparseCore 0:
  13.9 123.6 all-gather.3
  166.1 33.9 all-gather.5
  222.8 37.7 reduce-scatter.1
  264.0 31.0 all-gather.7
where the time goes:
time: 370 us
  waiting for transfers between devices  247 us (67%)
  matrix products  42.3 us (11%)
  local copies, waits for them, and re-layouts  36.7 us (10%)
  other arithmetic  16.7 us (5%)
  between operations  15.3 us (4%)
  starting transfers between devices  11.6 us (3%)
    all_gather x1, waiting for transfers between devices, body(): all_kv = lax.all_gather(own_kv, 'tok', axis=0, tiled=True)  112 us
    reduce_scatter x1, waiting for transfers between devices, body(): lax.psum_scatter(jnp.dot(hidden, down_weight, preferred_element_type=jnp....  37.9 us
    all_gather x1, waiting for transfers between devices, body(): gathered = lax.all_gather(residual_mid, 'req', axis=0, tiled=True)  33.9 us
    all_gather x1, waiting for transfers between devices, body(): lax.all_gather(next_normed, 'req', axis=0, tiled=True)  31.2 us
    all_to_all x1, waiting for transfers between devices, body(): lax.all_to_all(projected_cols, 'req', split_axis=0, concat_axis=1, tiled=...  18.2 us
    all_to_all x1, waiting for transfers between devices, body(): lax.all_to_all(outgoing, 'tok', split_axis=0, concat_axis=0, tiled=True)  14.1 us
    dot_general x1, matrix products, body(): jnp.dot(hidden, down_weight, preferred_element_type=jnp.float32)  12.4 us
    dot_general x1, matrix products, body(): jnp.einsum('hmqk,khe->hmqe', weights.astype(jnp.bfloat16), value_split, p...  8.27 us
  transfers between devices with their start and end apart: 6, of which 6 were waited for; matrix products, arithmetic and copies ran while one was open for 5% of the time, Pallas kernels for 0%

commit v1 on v0

--- a/solution.py
+++ b/solution.py
@@ -54,7 +54,24 @@
     run_max = jnp.full((HEADS, 2, row_count), NEG_FILL, jnp.float32)
     back = -(-(MAX_SEG - 1) // row_count)
     own_kv = jnp.concatenate([k_in, v_in], axis=1)
-    all_kv = lax.all_gather(own_kv, "tok", axis=0, tiled=True)
+    peers, position, rows = (lax.axis_size("tok"), lax.axis_index("tok"), own_kv.shape[0])
+    ahead = [(i, (i + 1) % peers) for i in range(peers)]
+    left = [(i, (i - 1) % peers) for i in range(peers)]
+    out = jnp.zeros((*own_kv.shape[:0], peers * rows, *own_kv.shape[0 + 1 :]), own_kv.dtype)
+    out = lax.dynamic_update_slice_in_dim(out, own_kv, position * rows, axis=0)
+    from_left = from_right = own_kv
+    half = peers // 2
+    for step in range(1, half + 1):
+        from_left = lax.ppermute(from_left, "tok", ahead)
+        out = lax.dynamic_update_slice_in_dim(
+            out, from_left, (position - step) % peers * rows, axis=0
+        )
+        if step < peers - half:
+            from_right = lax.ppermute(from_right, "tok", left)
+            out = lax.dynamic_update_slice_in_dim(
+                out, from_right, (position + step) % peers * rows, axis=0
+            )
+    all_kv = out
     padded_kv = jnp.concatenate(
         [jnp.zeros((back * row_count, 2 * feat_width), all_kv.dtype), all_kv], axis=0
     )

time: 370 us -> 458 us (1.24)
  starting transfers between devices: 11.6 us -> 51.7 us
  local copies, waits for them, and re-layouts: 36.7 us -> 70.2 us
  waiting for transfers between devices: 247 us -> 260 us
    ppermute x0 -> x15, waiting for transfers between devices: none -> 129 us  [the longest x8 122 us: body(): from_left = lax.ppermute(from_left, 'tok', ahead)]
    all_gather x1 -> x0, waiting for transfers between devices: 112 us -> none  [body(): all_kv = lax.all_gather(own_kv, 'tok', axis=0, tiled=True)]
    ppermute x0 -> x15, starting transfers between devices: none -> 40 us  [the longest x7 38 us: body(): from_right = lax.ppermute(from_right, 'tok', left)]
    dynamic_update_slice x0 -> x15, local copies, waits for them, and re-layouts: none -> 25.4 us  [the longest x8 13.9 us: body(): lax.dynamic_update_slice_in_dim(out, from_left, (position - step) % peers...]
    broadcast_in_dim x0 -> x1, local copies, waits for them, and re-layouts: none -> 5.97 us  [body(): jnp.zeros((*own_kv.shape[:0], peers * rows, *own_kv.shape[0 + 1:]), own_k...]
    unnamed x28 -> x30, local copies, waits for them, and re-layouts: 8.25 us -> 10.3 us
  transfers between devices with their start and end apart: 6 -> 20, of which waited for: 6 -> 18; matrix products, arithmetic and copies ran while one was open for 5% -> 9% of each run, Pallas kernels for 0% -> 0%
where the time goes in v1:
time: 458 us; the launch traced here: 457 us
  waiting for transfers between devices  260 us (57%)
  local copies, waits for them, and re-layouts  70.2 us (15%)
  starting transfers between devices  51.7 us (11%)
  matrix products  43.6 us (10%)
  between operations  15.6 us (3%)
  other arithmetic  15.4 us (3%)
    ppermute x8, waiting for transfers between devices, body(): from_left = lax.ppermute(from_left, 'tok', ahead)  122 us
    ppermute x7, starting transfers between devices, body(): from_right = lax.ppermute(from_right, 'tok', left)  38 us
    reduce_scatter x1, waiting for transfers between devices, body(): lax.psum_scatter(jnp.dot(hidden, down_weight, preferred_element_type=jnp....  37.9 us
    all_gather x1, waiting for transfers between devices, body(): lax.all_gather(next_normed, 'req', axis=0, tiled=True)  31.2 us
    all_gather x1, waiting for transfers between devices, body(): gathered = lax.all_gather(residual_mid, 'req', axis=0, tiled=True)  30 us
    all_to_all x1, waiting for transfers between devices, body(): lax.all_to_all(projected_cols, 'req', split_axis=0, concat_axis=1, tiled=...  18.2 us
    all_to_all x1, waiting for transfers between devices, body(): lax.all_to_all(outgoing, 'tok', split_axis=0, concat_axis=0, tiled=True)  14.1 us
    dynamic_update_slice x8, local copies, waits for them, and re-layouts, body(): lax.dynamic_update_slice_in_dim(out, from_left, (position - step) % peers...  13.9 us
  transfers between devices with their start and end apart: 20, of which 18 were waited for; matrix products, arithmetic and copies ran while one was open for 9% of the time, Pallas kernels for 0%

profile of v1, /device:TPU:0, one launch (start us, length us, event | category | flops | bytes accessed | tf_op | source)
XLA Modules:
  0.0 456.8 jit_solution(4919232238997511249)
XLA Ops:
  11.5 6.0 %broadcast_in_dim.64 = bf16[2048,4096]{0,1:T(8,128)(2,1)} broadcast(bf16[]{:T(256)} %constant.151.clone.1), dimensions={} | broadcast | bytes 16777218 | tf_op jit(solution)/shard_map/broadcast_in_dim | solution.py:60
  25.0 23.3 %collective-permute-done = bf16[128,4096]{0,1:T(8,128)(2,1)} collective-permute-done((bf16[128,4096]{0,1:T(8,128)(2,1)S(1)}, bf16[128,4096]{0,1:T(8,128)(2,1)}, u32[]{:S(2)}, u32[]{:S(2)}) %collective-permute-start) | collective-permute-done | bytes 1048608 | tf_op jit(solution)/shard_map/ppermute | solution.py:65
  53.6 22.6 %collective-permute-done.2 = bf16[128,4096]{0,1:T(8,128)(2,1)} collective-permute-done((bf16[128,4096]{0,1:T(8,128)(2,1)}, bf16[128,4096]{0,1:T(8,128)(2,1)}, u32[]{:S(2)}, u32[]{:S(2)}) %collective-permute-start.2) | collective-permute-done | bytes 1048608 | tf_op jit(solution)/shard_map/ppermute | solution.py:65
  76.4 6.5 %gather_fusion = s32[1152]{0:T(1024)S(1)} fusion(s32[2048]{0:T(1024)S(1)} %bitcast.64, s32[2048]{0:T(1024)S(1)} %pad_clamp_fusion), kind=kCustom, calls=%fused_computation | custom fusion | bytes 13824 | tf_op jit(solution)/shard_map/jit(_take)/gather | solution.py:85
  91.4 11.8 %collective-permute-done.4 = bf16[128,4096]{0,1:T(8,128)(2,1)} collective-permute-done((bf16[128,4096]{0,1:T(8,128)(2,1)}, bf16[128,4096]{0,1:T(8,128)(2,1)}, u32[]{:S(2)}, u32[]{:S(2)}) %collective-permute-start.4) | collective-permute-done | bytes 1048608 | tf_op jit(solution)/shard_map/ppermute | solution.py:65
  109.2 5.8 %collective-permute-start.7 = (bf16[128,4096]{0,1:T(8,128)(2,1)}, bf16[128,4096]{0,1:T(8,128)(2,1)S(1)}, u32[]{:S(2)}, u32[]{:S(2)}) collective-permute-start(bf16[128,4096]{0,1:T(8,128)(2,1)} %collective-permute-done.5), channel_id=1, source_target_pairs={{0,15},{1,0},{2,1},{3,2},{4,3},{5,4},{6,5},{7,6},{8,7},{9,8},{10,9... | collective-permute-start | bytes 3145736 | tf_op jit(solution)/shard_map/ppermute | solution.py:70
  117.3 12.1 %collective-permute-done.6 = bf16[128,4096]{0,1:T(8,128)(2,1)} collective-permute-done((bf16[128,4096]{0,1:T(8,128)(2,1)}, bf16[128,4096]{0,1:T(8,128)(2,1)}, u32[]{:S(2)}, u32[]{:S(2)}) %collective-permute-start.6) | collective-permute-done | bytes 1048608 | tf_op jit(solution)/shard_map/ppermute | solution.py:65
  135.0 5.7 %collective-permute-start.9 = (bf16[128,4096]{0,1:T(8,128)(2,1)S(1)}, bf16[128,4096]{0,1:T(8,128)(2,1)S(1)}, u32[]{:S(2)}, u32[]{:S(2)}) collective-permute-start(bf16[128,4096]{0,1:T(8,128)(2,1)S(1)} %collective-permute-done.7), channel_id=1, source_target_pairs={{0,15},{1,0},{2,1},{3,2},{4,3},{5,4},{6,5},{7,6},{8,7},{9,8},{10,9... | collective-permute-start | bytes 3145736 | tf_op jit(solution)/shard_map/ppermute | solution.py:70
  143.1 11.5 %collective-permute-done.8 = bf16[128,4096]{0,1:T(8,128)(2,1)S(1)} collective-permute-done((bf16[128,4096]{0,1:T(8,128)(2,1)}, bf16[128,4096]{0,1:T(8,128)(2,1)S(1)}, u32[]{:S(2)}, u32[]{:S(2)}) %collective-permute-start.8) | collective-permute-done | bytes 1048608 | tf_op jit(solution)/shard_map/ppermute | solution.py:65
  159.5 5.8 %collective-permute-start.11 = (bf16[128,4096]{0,1:T(8,128)(2,1)S(1)}, bf16[128,4096]{0,1:T(8,128)(2,1)S(1)}, u32[]{:S(2)}, u32[]{:S(2)}) collective-permute-start(bf16[128,4096]{0,1:T(8,128)(2,1)S(1)} %collective-permute-done.9), channel_id=1, source_target_pairs={{0,15},{1,0},{2,1},{3,2},{4,3},{5,4},{6,5},{7,6},{8,7},{9,8},{10,9... | collective-permute-start | bytes 3145736 | tf_op jit(solution)/shard_map/ppermute | solution.py:70
  166.5 12.0 %collective-permute-done.10 = bf16[128,4096]{0,1:T(8,128)(2,1)S(1)} collective-permute-done((bf16[128,4096]{0,1:T(8,128)(2,1)S(1)}, bf16[128,4096]{0,1:T(8,128)(2,1)S(1)}, u32[]{:S(2)}, u32[]{:S(2)}) %collective-permute-start.10) | collective-permute-done | bytes 1048608 | tf_op jit(solution)/shard_map/ppermute | solution.py:65
  183.2 5.8 %collective-permute-start.13 = (bf16[128,4096]{0,1:T(8,128)(2,1)S(1)}, bf16[128,4096]{0,1:T(8,128)(2,1)S(1)}, u32[]{:S(2)}, u32[]{:S(2)}) collective-permute-start(bf16[128,4096]{0,1:T(8,128)(2,1)S(1)} %collective-permute-done.11), channel_id=1, source_target_pairs={{0,15},{1,0},{2,1},{3,2},{4,3},{5,4},{6,5},{7,6},{8,7},{9,8},{10,9... | collective-permute-start | bytes 3145736 | tf_op jit(solution)/shard_map/ppermute | solution.py:70
  190.2 11.7 %collective-permute-done.12 = bf16[128,4096]{0,1:T(8,128)(2,1)S(1)} collective-permute-done((bf16[128,4096]{0,1:T(8,128)(2,1)S(1)}, bf16[128,4096]{0,1:T(8,128)(2,1)S(1)}, u32[]{:S(2)}, u32[]{:S(2)}) %collective-permute-start.12) | collective-permute-done | bytes 1048608 | tf_op jit(solution)/shard_map/ppermute | solution.py:65
  207.1 16.9 %collective-permute-done.14 = bf16[128,4096]{0,1:T(8,128)(2,1)S(1)} collective-permute-done((bf16[128,4096]{0,1:T(8,128)(2,1)S(1)}, bf16[128,4096]{0,1:T(8,128)(2,1)S(1)}, u32[]{:S(2)}, u32[]{:S(2)}) %collective-permute-start.14) | collective-permute-done | bytes 1048608 | tf_op jit(solution)/shard_map/ppermute | solution.py:65
  238.6 8.3 %broadcast_divide_fusion = f32[8,2,128,256]{3,2,1,0:T(8,128)S(1)} fusion(f32[8,2,128]{2,1,0:T(2,128)S(1)} %fusion.4, bf16[1152,8,256,1]{0,2,3,1:T(8,128)(2,1)} %bitcast.68, f32[8,2,1152,128]{3,2,1,0:T(8,128)} %copy-done.2, f32[8,2,128]{2,1,0:T(2,128)S(1)} %broadcast_maximum_fusion, pred[128,1152]{0,1:T(8,128)(4,1)S(1)} %compare_and_fusion), kind=kOutput, calls=%fused_computation.41 | convolution fusion | flops 1220280320 | bytes 16416768 | tf_op jit(solution)/shard_map/hmqk,khe->hmqe/dot_general | solution.py:99
  256.2 30.0 %all-gather.3.cloned.1.call-done = bf16[1024,2048]{1,0:T(8,128)(2,1)} async-done(((bf16[128,2048]{1,0:T(8,128)(2,1)}), bf16[1024,2048]{1,0:T(8,128)(2,1)}) %all-gather.3.cloned.1.call-update) | async-done | bytes 4194320 | tf_op jit(solution)/shard_map/all_gather | solution.py:116
  289.3 8.0 %fusion.15 = f32[1024,704]{0,1:T(8,128)} fusion(bf16[2048,704]{0,1:T(8,128)(2,1)} %param.23, bf16[1024,2048]{1,0:T(8,128)(2,1)} %all-gather.3.cloned.1.call-done, f32[2048]{0:T(1024)S(1)} %copy-done.12, f32[1024]{0:T(1024)S(1)} %add_rsqrt_fusion), kind=kOutput, calls=%fused_computation.29 | convolution fusion | flops 2961178624 | bytes 9973760 | tf_op jit(solution)/shard_map/dot_general | solution.py:118
  297.3 12.4 %convolution_convert_fusion = bf16[1024,2048]{1,0:T(8,128)(2,1)} fusion(bf16[704,2048]{1,0:T(8,128)(2,1)} %param.25, f32[1024,704]{0,1:T(8,128)} %fusion.15, bf16[2048,704]{0,1:T(8,128)(2,1)} %param.24, bf16[1024,2048]{1,0:T(8,128)(2,1)} %all-gather.3.cloned.1.call-done, f32[2048]{0:T(1024)S(1)} %copy-done.12, f32[1024]{0:T(1024)S(1)} %add_rsqrt_fusion), kind=kOutput, calls=%fused_computation.22 | convolution fusion | flops 5920391168 | bytes 17051648 | tf_op jit(solution)/shard_map/dot_general | solution.py:122
  309.8 37.9 %reduce-scatter.2.cloned.1.call-done = bf16[128,2048]{1,0:T(8,128)(2,1)} async-done(((bf16[1024,2048]{1,0:T(8,128)(2,1)}), bf16[128,2048]{1,0:T(8,128)(2,1)}) %reduce-scatter.2.cloned.1.call-update) | async-done | bytes 524304 | tf_op jit(solution)/shard_map/reduce_scatter | solution.py:121
  350.9 31.2 %all-gather.5.cloned.1.call-done = bf16[1024,2048]{1,0:T(8,128)(2,1)} async-done(((bf16[128,2048]{1,0:T(8,128)(2,1)}), bf16[1024,2048]{1,0:T(8,128)(2,1)}) %all-gather.5.cloned.1.call-update) | async-done | bytes 4194320 | tf_op jit(solution)/shard_map/all_gather | solution.py:130
  382.1 6.8 %convolution_convert_fusion.1 = bf16[1024,768]{1,0:T(8,128)(2,1)} fusion(bf16[1024,2048]{1,0:T(8,128)(2,1)} %all-gather.5.cloned.1.call-done, bf16[2048,768]{1,0:T(8,128)(2,1)S(1)} %copy-done), kind=kOutput, calls=%fused_computation.26 | convolution fusion | flops 3222011904 | bytes 8912896 | tf_op jit(solution)/shard_map/dot_general | solution.py:129
  396.6 18.2 %all-to-all-done = bf16[8,128,768]{2,1,0:T(8,128)(2,1)} async-done(((bf16[8,128,768]{2,1,0:T(8,128)(2,1)}), bf16[8,128,768]{2,1,0:T(8,128)(2,1)}, u32[]{:S(2)}, u32[]{:S(2)}) %all-to-all-start) | async-done | bytes 1572896 | tf_op jit(solution)/shard_map/all_to_all | solution.py:134
  421.4 7.0 %all-to-all-start.1 = ((bf16[16,1,8,4096]{3,2,1,0:T(8,128)(2,1)}), bf16[16,1,8,4096]{3,2,1,0:T(8,128)(2,1)}, u32[]{:S(2)}, u32[]{:S(2)}) async-start(bf16[16,1,8,4096]{3,2,1,0:T(8,128)(2,1)} %bitcast.69), calls=%async_computation.2 | async-start | bytes 2097152 | tf_op jit(solution)/shard_map/all_to_all | solution.py:145
  431.7 14.1 %all-to-all-done.1 = bf16[16,1,8,4096]{3,2,1,0:T(8,128)(2,1)} async-done(((bf16[16,1,8,4096]{3,2,1,0:T(8,128)(2,1)}), bf16[16,1,8,4096]{3,2,1,0:T(8,128)(2,1)}, u32[]{:S(2)}, u32[]{:S(2)}) %all-to-all-start.1) | async-done | bytes 1048608 | tf_op jit(solution)/shard_map/all_to_all | solution.py:145
  (119 shorter events, 110.0 us)
Async XLA Ops:
  7.2 375.0 %copy-start = (bf16[2048,768]{1,0:T(8,128)(2,1)S(1)}, bf16[2048,768]{1,0:T(8,128)(2,1)}, u32[]{:S(2)}) copy-start(bf16[2048,768]{1,0:T(8,128)(2,1)} %param.27) | copy-start | bytes 9437188
  7.2 279.0 %all-gather.3.cloned.1.call-start = ((), (), s32[]{:S(2)}) async-start(), calls=%async_computation.3 | async-start | bytes 4718592 | tf_op jit(solution)/shard_map/all_gather | solution.py:116
  11.5 64.9 %copy-start.1 = (s32[1,2048]{1,0:T(1,128)S(1)}, s32[1,2048]{1,0:T(1,128)}, u32[]{:S(2)}) copy-start(s32[1,2048]{1,0:T(1,128)} %param.19) | copy-start | bytes 24580
  17.4 85.8 %copy-start.9 = (f32[4,128]{1,0:T(4,128)S(1)}, f32[4,128]{1,0:T(4,128)}, u32[]{:S(2)}) copy-start(f32[4,128]{1,0:T(4,128)} %param.20) | copy-start | bytes 6148
  18.7 29.6 %collective-permute-start = (bf16[128,4096]{0,1:T(8,128)(2,1)S(1)}, bf16[128,4096]{0,1:T(8,128)(2,1)}, u32[]{:S(2)}, u32[]{:S(2)}) collective-permute-start(bf16[128,4096]{0,1:T(8,128)(2,1)S(1)} %get-tuple-element.13), channel_id=1, source_target_pairs={{0,1},{1,2},{2,3},{3,4},{4,5},{5,6},{6,7},{7,8},{8,9},{9,10},{10,1... | collective-permute-start | bytes 3145736 | tf_op jit(solution)/shard_map/ppermute | solution.py:65
  20.7 27.6 %collective-permute-start.1 = (bf16[128,4096]{0,1:T(8,128)(2,1)S(1)}, bf16[128,4096]{0,1:T(8,128)(2,1)}, u32[]{:S(2)}, u32[]{:S(2)}) collective-permute-start(bf16[128,4096]{0,1:T(8,128)(2,1)S(1)} %get-tuple-element.13), channel_id=1, source_target_pairs={{0,15},{1,0},{2,1},{3,2},{4,3},{5,4},{6,5},{7,6},{8,7},{9,8},{10,9... | collective-permute-start | bytes 3145736 | tf_op jit(solution)/shard_map/ppermute | solution.py:70
  48.2 28.0 %collective-permute-start.2 = (bf16[128,4096]{0,1:T(8,128)(2,1)}, bf16[128,4096]{0,1:T(8,128)(2,1)}, u32[]{:S(2)}, u32[]{:S(2)}) collective-permute-start(bf16[128,4096]{0,1:T(8,128)(2,1)} %collective-permute-done), channel_id=1, source_target_pairs={{0,1},{1,2},{2,3},{3,4},{4,5},{5,6},{6,7},{7,8},{8,9},{9,10},{10,1... | collective-permute-start | bytes 3145736 | tf_op jit(solution)/shard_map/ppermute | solution.py:65
  48.2 34.7 %collective-permute-start.3 = (bf16[128,4096]{0,1:T(8,128)(2,1)}, bf16[128,4096]{0,1:T(8,128)(2,1)}, u32[]{:S(2)}, u32[]{:S(2)}) collective-permute-start(bf16[128,4096]{0,1:T(8,128)(2,1)} %collective-permute-done.1), channel_id=1, source_target_pairs={{0,15},{1,0},{2,1},{3,2},{4,3},{5,4},{6,5},{7,6},{8,7},{9,8},{10,9... | collective-permute-start | bytes 3145736 | tf_op jit(solution)/shard_map/ppermute | solution.py:70
  76.2 27.1 %collective-permute-start.4 = (bf16[128,4096]{0,1:T(8,128)(2,1)}, bf16[128,4096]{0,1:T(8,128)(2,1)}, u32[]{:S(2)}, u32[]{:S(2)}) collective-permute-start(bf16[128,4096]{0,1:T(8,128)(2,1)} %collective-permute-done.2), channel_id=1, source_target_pairs={{0,1},{1,2},{2,3},{3,4},{4,5},{5,6},{6,7},{7,8},{8,9},{9,10},{10,1... | collective-permute-start | bytes 3145736 | tf_op jit(solution)/shard_map/ppermute | solution.py:65
  82.9 26.2 %collective-permute-start.5 = (bf16[128,4096]{0,1:T(8,128)(2,1)}, bf16[128,4096]{0,1:T(8,128)(2,1)}, u32[]{:S(2)}, u32[]{:S(2)}) collective-permute-start(bf16[128,4096]{0,1:T(8,128)(2,1)} %collective-permute-done.3), channel_id=1, source_target_pairs={{0,15},{1,0},{2,1},{3,2},{4,3},{5,4},{6,5},{7,6},{8,7},{9,8},{10,9... | collective-permute-start | bytes 3145736 | tf_op jit(solution)/shard_map/ppermute | solution.py:70
  103.3 26.1 %collective-permute-start.6 = (bf16[128,4096]{0,1:T(8,128)(2,1)}, bf16[128,4096]{0,1:T(8,128)(2,1)}, u32[]{:S(2)}, u32[]{:S(2)}) collective-permute-start(bf16[128,4096]{0,1:T(8,128)(2,1)} %collective-permute-done.4), channel_id=1, source_target_pairs={{0,1},{1,2},{2,3},{3,4},{4,5},{5,6},{6,7},{7,8},{8,9},{9,10},{10,1... | collective-permute-start | bytes 3145736 | tf_op jit(solution)/shard_map/ppermute | solution.py:65
  109.2 25.9 %collective-permute-start.7 = (bf16[128,4096]{0,1:T(8,128)(2,1)}, bf16[128,4096]{0,1:T(8,128)(2,1)S(1)}, u32[]{:S(2)}, u32[]{:S(2)}) collective-permute-start(bf16[128,4096]{0,1:T(8,128)(2,1)} %collective-permute-done.5), channel_id=1, source_target_pairs={{0,15},{1,0},{2,1},{3,2},{4,3},{5,4},{6,5},{7,6},{8,7},{9,8},{10,9... | collective-permute-start | bytes 3145736 | tf_op jit(solution)/shard_map/ppermute | solution.py:70
  129.4 25.1 %collective-permute-start.8 = (bf16[128,4096]{0,1:T(8,128)(2,1)}, bf16[128,4096]{0,1:T(8,128)(2,1)S(1)}, u32[]{:S(2)}, u32[]{:S(2)}) collective-permute-start(bf16[128,4096]{0,1:T(8,128)(2,1)} %collective-permute-done.6), channel_id=1, source_target_pairs={{0,1},{1,2},{2,3},{3,4},{4,5},{5,6},{6,7},{7,8},{8,9},{9,10},{10,1... | collective-permute-start | bytes 3145736 | tf_op jit(solution)/shard_map/ppermute | solution.py:65
  135.0 24.5 %collective-permute-start.9 = (bf16[128,4096]{0,1:T(8,128)(2,1)S(1)}, bf16[128,4096]{0,1:T(8,128)(2,1)S(1)}, u32[]{:S(2)}, u32[]{:S(2)}) collective-permute-start(bf16[128,4096]{0,1:T(8,128)(2,1)S(1)} %collective-permute-done.7), channel_id=1, source_target_pairs={{0,15},{1,0},{2,1},{3,2},{4,3},{5,4},{6,5},{7,6},{8,7},{9,8},{10,9... | collective-permute-start | bytes 3145736 | tf_op jit(solution)/shard_map/ppermute | solution.py:70
  154.5 24.0 %collective-permute-start.10 = (bf16[128,4096]{0,1:T(8,128)(2,1)S(1)}, bf16[128,4096]{0,1:T(8,128)(2,1)S(1)}, u32[]{:S(2)}, u32[]{:S(2)}) collective-permute-start(bf16[128,4096]{0,1:T(8,128)(2,1)S(1)} %collective-permute-done.8), channel_id=1, source_target_pairs={{0,1},{1,2},{2,3},{3,4},{4,5},{5,6},{6,7},{7,8},{8,9},{9,10},{10,1... | collective-permute-start | bytes 3145736 | tf_op jit(solution)/shard_map/ppermute | solution.py:65
  159.5 23.7 %collective-permute-start.11 = (bf16[128,4096]{0,1:T(8,128)(2,1)S(1)}, bf16[128,4096]{0,1:T(8,128)(2,1)S(1)}, u32[]{:S(2)}, u32[]{:S(2)}) collective-permute-start(bf16[128,4096]{0,1:T(8,128)(2,1)S(1)} %collective-permute-done.9), channel_id=1, source_target_pairs={{0,15},{1,0},{2,1},{3,2},{4,3},{5,4},{6,5},{7,6},{8,7},{9,8},{10,9... | collective-permute-start | bytes 3145736 | tf_op jit(solution)/shard_map/ppermute | solution.py:70
  178.5 23.3 %collective-permute-start.12 = (bf16[128,4096]{0,1:T(8,128)(2,1)S(1)}, bf16[128,4096]{0,1:T(8,128)(2,1)S(1)}, u32[]{:S(2)}, u32[]{:S(2)}) collective-permute-start(bf16[128,4096]{0,1:T(8,128)(2,1)S(1)} %collective-permute-done.10), channel_id=1, source_target_pairs={{0,1},{1,2},{2,3},{3,4},{4,5},{5,6},{6,7},{7,8},{8,9},{9,10},{10,1... | collective-permute-start | bytes 3145736 | tf_op jit(solution)/shard_map/ppermute | solution.py:65
  183.2 22.8 %collective-permute-start.13 = (bf16[128,4096]{0,1:T(8,128)(2,1)S(1)}, bf16[128,4096]{0,1:T(8,128)(2,1)S(1)}, u32[]{:S(2)}, u32[]{:S(2)}) collective-permute-start(bf16[128,4096]{0,1:T(8,128)(2,1)S(1)} %collective-permute-done.11), channel_id=1, source_target_pairs={{0,15},{1,0},{2,1},{3,2},{4,3},{5,4},{6,5},{7,6},{8,7},{9,8},{10,9... | collective-permute-start | bytes 3145736 | tf_op jit(solution)/shard_map/ppermute | solution.py:70
  201.8 22.2 %collective-permute-start.14 = (bf16[128,4096]{0,1:T(8,128)(2,1)S(1)}, bf16[128,4096]{0,1:T(8,128)(2,1)S(1)}, u32[]{:S(2)}, u32[]{:S(2)}) collective-permute-start(bf16[128,4096]{0,1:T(8,128)(2,1)S(1)} %collective-permute-done.12), channel_id=1, source_target_pairs={{0,1},{1,2},{2,3},{3,4},{4,5},{5,6},{6,7},{7,8},{8,9},{9,10},{10,1... | collective-permute-start | bytes 3145736 | tf_op jit(solution)/shard_map/ppermute | solution.py:65
  255.9 91.7 %reduce-scatter.2.cloned.1.call-start = ((), (), s32[]{:S(2)}) async-start(), calls=%async_computation.4 | async-start | bytes 4718592 | tf_op jit(solution)/shard_map/reduce_scatter | solution.py:121
  297.3 52.6 %copy-start.8 = (f32[2048]{0:T(1024)S(1)}, f32[2048]{0:T(1024)}, u32[]{:S(2)}) copy-start(f32[2048]{0:T(1024)} %param.26) | copy-start | bytes 24580
  309.7 72.4 %all-gather.5.cloned.1.call-start = ((), (), s32[]{:S(2)}) async-start(), calls=%async_computation.5 | async-start | bytes 4718592 | tf_op jit(solution)/shard_map/all_gather | solution.py:130
  388.9 25.9 %all-to-all-start = ((bf16[8,128,768]{2,1,0:T(8,128)(2,1)}), bf16[8,128,768]{2,1,0:T(8,128)(2,1)}, u32[]{:S(2)}, u32[]{:S(2)}) async-start(bf16[8,128,768]{2,1,0:T(8,128)(2,1)} %bitcast.71), calls=%async_computation.1 | async-start | bytes 3145728 | tf_op jit(solution)/shard_map/all_to_all | solution.py:134
  421.4 24.4 %all-to-all-start.1 = ((bf16[16,1,8,4096]{3,2,1,0:T(8,128)(2,1)}), bf16[16,1,8,4096]{3,2,1,0:T(8,128)(2,1)}, u32[]{:S(2)}, u32[]{:S(2)}) async-start(bf16[16,1,8,4096]{3,2,1,0:T(8,128)(2,1)} %bitcast.69), calls=%async_computation.2 | async-start | bytes 2097152 | tf_op jit(solution)/shard_map/all_to_all | solution.py:145
  (9 other events, 148.1 us)
Sparse Core Ops, SparseCore 0:
  256.1 30.0 all-gather.2
  309.8 37.7 reduce-scatter.1
  351.0 31.0 all-gather.4
